TPU v7x, 128 devices: a whole 4x4x4 slice. The times are simulated.
128 devices in a mesh: sector: 64 (over y, z, x_hi, core), lift: 2 (over x_lo).
Axes of the slice: x: 4 (x_hi: 2, x_lo: 2; x = x_hi * 2 + x_lo), y: 4, z: 4, core: 2. Of those that a mesh axis runs over, the one named last changes fastest.
Arguments:
- right_side: float32 [128, 262144], P('lift', 'sector'), may hold values from -40 to 40
- diagonal: float32 [262144], P('sector'), may hold values from 1.9 to 2.6
- coupling: float32 [262144], P('sector'), may hold values from 0.3 to 0.94
- local_inverse: bfloat16 [256, 1024, 2048], P('sector'), may hold values from -0.1 to 0.6
- coarse_basis: bfloat16 [256, 16, 1024], P('sector'), may hold values from -0.1875 to 0.1875
- coarse_inverse: float32 [4096, 4096], P('sector', 'lift'), may hold values from -8 to 12
Outputs:
- solution: float32 [128, 262144], P('lift', 'sector')
- residual: float32 [128, 262144], P('lift', 'sector')
All inputs are finite; a program needn't handle non-finite values.
Results may differ from a plain program's by a relative error of at most 0.019.
Values may be sent and summed in bfloat16 or wider, within the bound.
No kernel may reach another device: no remote copies, remote signals or barrier semaphores. Data moves between devices by JAX's collectives and lax.ppermute only.
A program may use at most 128 MiB of HBM per device.

v0:
```python
import jax
import jax.numpy as jnp
from jax import lax
from jax.sharding import PartitionSpec as P

SWEEPS = 4
OUTER = 2


def extended_2(block, sides, width):
    for axis, dim in sides:
        count = lax.axis_size(axis)
        forward = [(i, i + 1) for i in range(count - 1)]
        forward.append((count - 1, 0))
        backward = [(target, source) for source, target in forward]
        low = lax.ppermute(
            lax.slice_in_dim(block, block.shape[dim] - width, None, axis=dim), axis, forward
        )
        high = lax.ppermute(lax.slice_in_dim(block, 0, width, axis=dim), axis, backward)
        block = jnp.concatenate([low, block, high], axis=dim)
    return block


def apply_op(extended, diag_part, link_part):
    return diag_part * extended[:, 1:-1] - link_part * (extended[:, :-2] + extended[:, 2:])


def body(right_side, diagonal, coupling, local_inverse, coarse_basis, coarse_inverse):
    highest = lax.Precision.HIGHEST
    num_cases, num_rows = right_side.shape
    sub_count = local_inverse.shape[0]
    own_rows = local_inverse.shape[1]
    inv_order = local_inverse.shape[2]
    margin = (inv_order - own_rows) // 2
    mode_count = coarse_basis.shape[1]
    basis_wide = coarse_basis.astype(jnp.float32)

    def rim_op(field):
        extended = extended_2(field, (("sector", 1),), 1)
        return apply_op(extended, diagonal, coupling)

    def intersection(half_res):
        return extended_2(half_res, (("sector", 1),), margin)

    def correct(padded):
        windows = jnp.stack(
            [
                padded[:, index * own_rows : index * own_rows + inv_order]
                for index in range(sub_count)
            ]
        )
        products = jnp.einsum(
            "jco,jko->cjk", windows, local_inverse, preferred_element_type=jnp.float32
        )
        return products.reshape(num_cases, num_rows)

    solution = jnp.zeros_like(right_side)
    residual = right_side
    for outer_step in range(OUTER):
        update = correct(intersection(residual.astype(jnp.bfloat16)))
        for sweep in range(SWEEPS - 1):
            padded = intersection((residual - rim_op(update)).astype(jnp.bfloat16))
            update = update + correct(padded)
        coarse_res = (residual - rim_op(update)).astype(jnp.bfloat16)
        projected = jnp.einsum(
            "cjk,jmk->cjm",
            coarse_res.reshape(num_cases, sub_count, own_rows),
            coarse_basis,
            preferred_element_type=jnp.float32,
        ).reshape(num_cases, sub_count * mode_count)
        gathered = lax.all_gather(projected, "sector", axis=1, tiled=True)
        swapped = lax.all_to_all(
            gathered.astype(jnp.bfloat16), "lift", split_axis=1, concat_axis=0, tiled=True
        ).astype(gathered.dtype)
        coarse_sol = lax.psum_scatter(
            jnp.dot(swapped, coarse_inverse.T, precision=highest).astype(jnp.bfloat16),
            "lift",
            scatter_dimension=0,
            tiled=True,
        ).astype(jnp.float32)
        coarse_wide = coarse_sol.reshape(num_cases, sub_count, mode_count)
        update = update + jnp.einsum(
            "cjm,jmk->cjk", coarse_wide, basis_wide, precision=highest
        ).reshape(num_cases, num_rows)
        image = rim_op(update)
        totals = lax.psum(
            (jnp.sum(residual * image, axis=1), jnp.sum(image * image, axis=1)), "sector"
        )
        alpha = totals[0] / (totals[1] + 1e-06)
        solution = solution + alpha[:, None] * update
        residual = residual - alpha[:, None] * image
    return (solution, residual)


def solution(mesh):
    in_specs = (
        P("lift", "sector"),
        P("sector"),
        P("sector"),
        P("sector", None, None),
        P("sector", None, None),
        P("sector", "lift"),
    )
    out_specs = (P("lift", "sector"), P("lift", "sector"))
    return jax.shard_map(body, mesh=mesh, in_specs=in_specs, out_specs=out_specs, check_vma=False)
```

profile of v0, /device:TPU:0, one launch (start us, length us, event | category | flops | bytes accessed | tf_op | source)
XLA Modules:
  0.0 904.0 jit_solution(17733858493407089266)
XLA Ops:
  7.3 1.4 convert_element_type.47
  8.7 8.6 collective-permute-start.1
  17.3 1.9 collective-permute-done
  20.0 11.0 %convolution_bitcast_fusion.9 = f32[4,8,8,1024]{3,2,1,0:T(8,128)S(1)} fusion(bf16[4,1024,2048]{2,1,0:T(8,128)(2,1)} %param.9, bf16[1,64,2048]{2,1,0:T(8,128)(2,1)} %get-tuple-element.79, bf16[1,64,2048]{2,1,0:T(8,128)(2,1)S(1)} %get-tuple-element.77, bf16[1,64,2048]{2,1,0:T(8,128)(2,1)S(1)} %get-tuple-element.78, bf16[1,64,2048]{2,1,0:T(8,128)(2,1)S(1)} %get-tuple-element.76), kind=kOutput, calls=%fused_computation.9 | convolution fusion | flops 1075314688 | bytes 18874368 | tf_op jit(solution)/shard_map/jco,jko->cjk/dot_general | solution.py:52
  31.3 7.6 collective-permute-start.3
  38.9 1.5 collective-permute-done.2
  41.3 7.5 collective-permute-start.5
  48.8 1.9 collective-permute-done.4
  51.5 11.1 %convolution_bitcast_fusion.8 = f32[4,8,8,1024]{3,2,1,0:T(8,128)S(1)} fusion(bf16[4,1024,2048]{2,1,0:T(8,128)(2,1)} %param.9, bf16[1,64,2048]{2,1,0:T(8,128)(2,1)} %get-tuple-element.73, bf16[1,64,2048]{2,1,0:T(8,128)(2,1)S(1)} %get-tuple-element.71, bf16[1,64,2048]{2,1,0:T(8,128)(2,1)S(1)} %get-tuple-element.72, bf16[1,64,2048]{2,1,0:T(8,128)(2,1)S(1)} %get-tuple-element.70), kind=kOutput, calls=%fused_computation.8 | convolution fusion | flops 1075314688 | bytes 18874368 | tf_op jit(solution)/shard_map/jco,jko->cjk/dot_general | solution.py:52
  62.7 1.3 add.76
  64.1 7.8 collective-permute-start.7
  74.3 7.5 collective-permute-start.9
  81.9 1.9 collective-permute-done.8
  84.6 12.0 %convolution_bitcast_fusion.7 = f32[4,8,8,1024]{3,2,1,0:T(8,128)} fusion(bf16[4,1024,2048]{2,1,0:T(8,128)(2,1)} %param.9, bf16[1,64,2048]{2,1,0:T(8,128)(2,1)} %get-tuple-element.67, bf16[1,64,2048]{2,1,0:T(8,128)(2,1)S(1)} %get-tuple-element.65, bf16[1,64,2048]{2,1,0:T(8,128)(2,1)S(1)} %get-tuple-element.66, bf16[1,64,2048]{2,1,0:T(8,128)(2,1)S(1)} %get-tuple-element.64), kind=kOutput, calls=%fused_computation.7 | convolution fusion | flops 1075314688 | bytes 18874368 | tf_op jit(solution)/shard_map/jco,jko->cjk/dot_general | solution.py:52
  96.6 1.3 copy.95
  98.2 7.6 collective-permute-start.11
  105.7 1.5 collective-permute-done.10
  108.1 7.5 collective-permute-start.13
  115.7 1.9 collective-permute-done.12
  118.4 12.0 %convolution_bitcast_fusion.6 = f32[4,8,8,1024]{3,2,1,0:T(8,128)} fusion(bf16[4,1024,2048]{2,1,0:T(8,128)(2,1)} %param.9, bf16[1,64,2048]{2,1,0:T(8,128)(2,1)} %get-tuple-element.61, bf16[1,64,2048]{2,1,0:T(8,128)(2,1)S(1)} %get-tuple-element.59, bf16[1,64,2048]{2,1,0:T(8,128)(2,1)S(1)} %get-tuple-element.60, bf16[1,64,2048]{2,1,0:T(8,128)(2,1)S(1)} %get-tuple-element.58), kind=kOutput, calls=%fused_computation.6 | convolution fusion | flops 1075314688 | bytes 18874368 | tf_op jit(solution)/shard_map/jco,jko->cjk/dot_general | solution.py:52
  130.5 1.3 copy.96
  132.0 16.4 %collective-permute-start.15 = (f32[64,1]{1,0:T(8,128)S(1)}, f32[64,1]{1,0:T(8,128)S(1)}, u32[]{:S(2)}, u32[]{:S(2)}) collective-permute-start(f32[64,1]{1,0:T(8,128)S(1)} %get-tuple-element.27), channel_id=1, source_target_pairs={{2,0},{4,2},{6,4},{8,6},{10,8},{12,10},{14,12},{16,14},{18,16},{20... | collective-permute-start | bytes 776 | tf_op jit(solution)/shard_map/ppermute | solution.py:19
  148.4 1.6 collective-permute-done.15
  151.8 92.6 %all_gather.6 = bf16[64,4096]{0,1:T(8,128)(2,1)S(1)} all-gather(bf16[64,64]{0,1:T(8,128)(2,1)S(1)} %bitcast.176), channel_id=1, replica_groups=mesh['sector'=64,'lift'=2] {'sector'}, dimensions={1}, use_global_device_ids=true | all-gather | bytes 532480 | tf_op jit(solution)/shard_map/all_gather | solution.py:71
  244.8 11.2 %all_to_all.38 = bf16[64,2,2048]{2,0,1:T(8,128)(2,1)S(1)} all-to-all(bf16[64,2,2048]{2,0,1:T(8,128)(2,1)S(1)} %bitcast.168), channel_id=1, replica_groups=mesh['sector'=64,'lift'=2] {'lift'}, dimensions={1} | all-to-all | bytes 1048576 | tf_op jit(solution)/shard_map/all_to_all | solution.py:72
  257.3 9.2 %reduce-scatter.3.cloned.1.call-done = bf16[64,64]{1,0:T(8,128)(2,1)} async-done(((bf16[128,64]{1,0:T(8,128)(2,1)}), bf16[64,64]{1,0:T(8,128)(2,1)}) %reduce-scatter.3.cloned.1.call-update) | async-done | bytes 8208 | tf_op jit(solution)/shard_map/reduce_scatter | solution.py:75
  268.6 1.3 add.82
  270.0 7.5 collective-permute-start.17
  277.5 1.6 collective-permute-done.16
  279.9 170.0 %all-reduce.1 = (f32[64]{0:T(128)S(1)}, f32[64]{0:T(128)S(1)}) all-reduce(f32[64]{0:T(128)S(1)} %get-tuple-element.5, f32[64]{0:T(128)S(1)} %get-tuple-element.4), channel_id=1, replica_groups=mesh['sector'=64,'lift'=2] {'sector'}, use_global_device_ids=true, to_apply=%region_2.0 | all-reduce | flops 128 | bytes 1024 | tf_op jit(solution)/shard_map/psum | solution.py:86
  449.9 2.6 fusion.132
  452.6 7.5 collective-permute-start.19
  460.0 1.9 collective-permute-done.18
  462.1 11.9 %convolution_bitcast_fusion.4 = f32[4,8,8,1024]{3,2,1,0:T(8,128)} fusion(bf16[4,1024,2048]{2,1,0:T(8,128)(2,1)} %param.9, bf16[1,64,2048]{2,1,0:T(8,128)(2,1)S(1)} %get-tuple-element.55, bf16[1,64,2048]{2,1,0:T(8,128)(2,1)S(1)} %get-tuple-element.53, bf16[1,64,2048]{2,1,0:T(8,128)(2,1)S(1)} %get-tuple-element.54, bf16[1,64,2048]{2,1,0:T(8,128)(2,1)S(1)} %get-tuple-element.52), kind=kOutput, calls=%fused_computation.4 | convolution fusion | flops 1075314688 | bytes 18874368 | tf_op jit(solution)/shard_map/jco,jko->cjk/dot_general | solution.py:52
  474.0 1.3 copy.98
  475.5 7.5 collective-permute-start.21
  483.0 1.5 collective-permute-done.20
  485.4 7.7 collective-permute-start.23
  493.1 1.7 collective-permute-done.22
  495.9 12.1 %convolution_bitcast_fusion.3 = f32[4,8,8,1024]{3,2,1,0:T(8,128)} fusion(bf16[4,1024,2048]{2,1,0:T(8,128)(2,1)} %param.9, bf16[1,64,2048]{2,1,0:T(8,128)(2,1)} %get-tuple-element.49, bf16[1,64,2048]{2,1,0:T(8,128)(2,1)S(1)} %get-tuple-element.47, bf16[1,64,2048]{2,1,0:T(8,128)(2,1)S(1)} %get-tuple-element.48, bf16[1,64,2048]{2,1,0:T(8,128)(2,1)S(1)} %get-tuple-element.46), kind=kOutput, calls=%fused_computation.3 | convolution fusion | flops 1075314688 | bytes 18874368 | tf_op jit(solution)/shard_map/jco,jko->cjk/dot_general | solution.py:52
  509.3 1.3 add.86
  510.7 7.6 collective-permute-start.25
  518.3 1.5 collective-permute-done.24
  520.7 7.5 collective-permute-start.27
  528.2 1.9 collective-permute-done.26
  530.9 12.0 %convolution_bitcast_fusion.2 = f32[4,8,8,1024]{3,2,1,0:T(8,128)} fusion(bf16[4,1024,2048]{2,1,0:T(8,128)(2,1)} %param.9, bf16[1,64,2048]{2,1,0:T(8,128)(2,1)} %get-tuple-element.43, bf16[1,64,2048]{2,1,0:T(8,128)(2,1)S(1)} %get-tuple-element.41, bf16[1,64,2048]{2,1,0:T(8,128)(2,1)S(1)} %get-tuple-element.42, bf16[1,64,2048]{2,1,0:T(8,128)(2,1)S(1)} %get-tuple-element.40), kind=kOutput, calls=%fused_computation.2 | convolution fusion | flops 1075314688 | bytes 18874368 | tf_op jit(solution)/shard_map/jco,jko->cjk/dot_general | solution.py:52
  544.5 7.6 collective-permute-start.29
  552.1 1.5 collective-permute-done.28
  554.5 7.8 collective-permute-start.31
  562.3 1.6 collective-permute-done.30
  564.3 12.0 %convolution_bitcast_fusion.1 = f32[4,8,8,1024]{3,2,1,0:T(8,128)} fusion(bf16[4,1024,2048]{2,1,0:T(8,128)(2,1)} %param.9, bf16[1,64,2048]{2,1,0:T(8,128)(2,1)S(1)} %get-tuple-element.37, bf16[1,64,2048]{2,1,0:T(8,128)(2,1)S(1)} %get-tuple-element.35, bf16[1,64,2048]{2,1,0:T(8,128)(2,1)S(1)} %get-tuple-element.36, bf16[1,64,2048]{2,1,0:T(8,128)(2,1)S(1)} %get-tuple-element.34), kind=kOutput, calls=%fused_computation.1 | convolution fusion | flops 1075314688 | bytes 18874368 | tf_op jit(solution)/shard_map/jco,jko->cjk/dot_general | solution.py:52
  576.3 1.4 copy.101
  577.7 1.3 add.90
  579.2 7.6 collective-permute-start.33
  586.7 1.5 collective-permute-done.32
  589.3 97.8 %all_gather.7 = bf16[64,4096]{0,1:T(8,128)(2,1)} all-gather(bf16[64,64]{0,1:T(8,128)(2,1)S(1)} %bitcast.177), channel_id=1, replica_groups=mesh['sector'=64,'lift'=2] {'sector'}, dimensions={1}, use_global_device_ids=true | all-gather | bytes 532480 | tf_op jit(solution)/shard_map/all_gather | solution.py:71
  687.1 1.5 copy.85
  688.7 11.2 %all_to_all.39 = bf16[64,2,2048]{2,0,1:T(8,128)(2,1)S(1)} all-to-all(bf16[64,2,2048]{2,0,1:T(8,128)(2,1)S(1)} %bitcast.170), channel_id=1, replica_groups=mesh['sector'=64,'lift'=2] {'lift'}, dimensions={1} | all-to-all | bytes 1048576 | tf_op jit(solution)/shard_map/all_to_all | solution.py:72
  701.1 9.2 %reduce-scatter.5.cloned.1.call-done = bf16[64,64]{1,0:T(8,128)(2,1)} async-done(((bf16[128,64]{1,0:T(8,128)(2,1)}), bf16[64,64]{1,0:T(8,128)(2,1)}) %reduce-scatter.5.cloned.1.call-update) | async-done | bytes 8208 | tf_op jit(solution)/shard_map/reduce_scatter | solution.py:75
  711.6 1.3 add.92
  713.0 7.5 collective-permute-start.35
  720.5 1.6 collective-permute-done.34
  722.9 170.0 %all-reduce = (f32[64]{0:T(128)S(1)}, f32[64]{0:T(128)S(1)}) all-reduce(f32[64]{0:T(128)S(1)} %get-tuple-element.3, f32[64]{0:T(128)S(1)} %get-tuple-element.2), channel_id=1, replica_groups=mesh['sector'=64,'lift'=2] {'sector'}, use_global_device_ids=true, to_apply=%region_7.0 | all-reduce | flops 128 | bytes 1024 | tf_op jit(solution)/shard_map/psum | solution.py:86
  892.8 3.9 multiply_subtract_fusion
  (129 shorter events, 27.5 us)
Async XLA Ops:
  7.2 248.8 %copy-start = (f32[64,2048]{1,0:T(8,128)S(1)}, f32[64,2048]{1,0:T(8,128)}, u32[]{:S(2)}) copy-start(f32[64,2048]{1,0:T(8,128)} %param.11) | copy-start | bytes 1572868
  7.2 33.3 %copy-start.1 = (f32[64,4096]{1,0:T(8,128)S(1)}, f32[64,4096]{1,0:T(8,128)}, u32[]{:S(2)}) copy-start(f32[64,4096]{1,0:T(8,128)} %param.6) | copy-start | bytes 3145732
  7.2 33.3 %copy-start.12 = (f32[4096]{0:T(1024)S(1)}, f32[4096]{0:T(1024)}, u32[]{:S(2)}) copy-start(f32[4096]{0:T(1024)} %param.8) | copy-start | bytes 49156
  7.2 33.3 %copy-start.13 = (f32[4096]{0:T(1024)S(1)}, f32[4096]{0:T(1024)}, u32[]{:S(2)}) copy-start(f32[4096]{0:T(1024)} %param.7) | copy-start | bytes 49156
  7.2 259.2 %reduce-scatter.3.cloned.1.call-start = ((), (), s32[]{:S(2)}) async-start(), calls=%async_computation.4 | async-start | bytes 49152 | tf_op jit(solution)/shard_map/reduce_scatter | solution.py:75
  8.7 10.5 %collective-permute-start = (bf16[64,512]{1,0:T(8,128)(2,1)S(1)}, bf16[64,512]{1,0:T(8,128)(2,1)S(1)}, u32[]{:S(2)}, u32[]{:S(2)}) collective-permute-start(bf16[64,512]{1,0:T(8,128)(2,1)S(1)} %get-tuple-element.80), channel_id=1, source_target_pairs={{0,2},{2,4},{4,6},{6,8},{8,10},{10,12},{12,14},{14,16},{16,18},{18... | collective-permute-start | bytes 196616 | tf_op jit(solution)/shard_map/ppermute | solution.py:16
  8.7 10.5 %collective-permute-start.1 = (bf16[64,512]{1,0:T(8,128)(2,1)S(1)}, bf16[64,512]{1,0:T(8,128)(2,1)S(1)}, u32[]{:S(2)}, u32[]{:S(2)}) collective-permute-start(bf16[64,512]{1,0:T(8,128)(2,1)S(1)} %get-tuple-element.81), channel_id=1, source_target_pairs={{2,0},{4,2},{6,4},{8,6},{10,8},{12,10},{14,12},{16,14},{18,16},{20... | collective-permute-start | bytes 196616 | tf_op jit(solution)/shard_map/ppermute | solution.py:19
  31.2 9.3 %copy-start.10 = (f32[4,8,8,1024]{3,2,0,1:T(8,128)}, f32[4,8,8,1024]{3,2,0,1:T(8,128)S(1)}, u32[]{:S(2)}) copy-start(f32[4,8,8,1024]{3,2,0,1:T(8,128)S(1)} %copy.93) | copy-start | bytes 3145732
  31.3 9.1 %collective-permute-start.2 = (f32[64,1]{1,0:T(8,128)S(1)}, f32[64,1]{1,0:T(8,128)S(1)}, u32[]{:S(2)}, u32[]{:S(2)}) collective-permute-start(f32[64,1]{1,0:T(8,128)S(1)} %get-tuple-element.32), channel_id=1, source_target_pairs={{0,2},{2,4},{4,6},{6,8},{8,10},{10,12},{12,14},{14,16},{16,18},{18... | collective-permute-start | bytes 776 | tf_op jit(solution)/shard_map/ppermute | solution.py:16
  31.3 9.2 %collective-permute-start.3 = (f32[64,1]{1,0:T(8,128)S(1)}, f32[64,1]{1,0:T(8,128)S(1)}, u32[]{:S(2)}, u32[]{:S(2)}) collective-permute-start(f32[64,1]{1,0:T(8,128)S(1)} %get-tuple-element.33), channel_id=1, source_target_pairs={{2,0},{4,2},{6,4},{8,6},{10,8},{12,10},{14,12},{16,14},{18,16},{20... | collective-permute-start | bytes 776 | tf_op jit(solution)/shard_map/ppermute | solution.py:19
  41.2 9.5 %collective-permute-start.4 = (bf16[64,512]{1,0:T(8,128)(2,1)S(1)}, bf16[64,512]{1,0:T(8,128)(2,1)S(1)}, u32[]{:S(2)}, u32[]{:S(2)}) collective-permute-start(bf16[64,512]{1,0:T(8,128)(2,1)S(1)} %get-tuple-element.74), channel_id=1, source_target_pairs={{0,2},{2,4},{4,6},{6,8},{8,10},{10,12},{12,14},{14,16},{16,18},{18... | collective-permute-start | bytes 196616 | tf_op jit(solution)/shard_map/ppermute | solution.py:16
  41.3 9.4 %collective-permute-start.5 = (bf16[64,512]{1,0:T(8,128)(2,1)S(1)}, bf16[64,512]{1,0:T(8,128)(2,1)S(1)}, u32[]{:S(2)}, u32[]{:S(2)}) collective-permute-start(bf16[64,512]{1,0:T(8,128)(2,1)S(1)} %get-tuple-element.75), channel_id=1, source_target_pairs={{2,0},{4,2},{6,4},{8,6},{10,8},{12,10},{14,12},{16,14},{18,16},{20... | collective-permute-start | bytes 196616 | tf_op jit(solution)/shard_map/ppermute | solution.py:19
  64.1 9.1 %collective-permute-start.6 = (f32[64,1]{1,0:T(8,128)S(1)}, f32[64,1]{1,0:T(8,128)S(1)}, u32[]{:S(2)}, u32[]{:S(2)}) collective-permute-start(f32[64,1]{1,0:T(8,128)S(1)} %get-tuple-element.30), channel_id=1, source_target_pairs={{0,2},{2,4},{4,6},{6,8},{8,10},{10,12},{12,14},{14,16},{16,18},{18... | collective-permute-start | bytes 776 | tf_op jit(solution)/shard_map/ppermute | solution.py:16
  64.1 9.4 %collective-permute-start.7 = (f32[64,1]{1,0:T(8,128)S(1)}, f32[64,1]{1,0:T(8,128)S(1)}, u32[]{:S(2)}, u32[]{:S(2)}) collective-permute-start(f32[64,1]{1,0:T(8,128)S(1)} %get-tuple-element.31), channel_id=1, source_target_pairs={{2,0},{4,2},{6,4},{8,6},{10,8},{12,10},{14,12},{16,14},{18,16},{20... | collective-permute-start | bytes 776 | tf_op jit(solution)/shard_map/ppermute | solution.py:19
  74.3 9.5 %collective-permute-start.8 = (bf16[64,512]{1,0:T(8,128)(2,1)S(1)}, bf16[64,512]{1,0:T(8,128)(2,1)S(1)}, u32[]{:S(2)}, u32[]{:S(2)}) collective-permute-start(bf16[64,512]{1,0:T(8,128)(2,1)S(1)} %get-tuple-element.68), channel_id=1, source_target_pairs={{0,2},{2,4},{4,6},{6,8},{8,10},{10,12},{12,14},{14,16},{16,18},{18... | collective-permute-start | bytes 196616 | tf_op jit(solution)/shard_map/ppermute | solution.py:16
  74.3 9.4 %collective-permute-start.9 = (bf16[64,512]{1,0:T(8,128)(2,1)S(1)}, bf16[64,512]{1,0:T(8,128)(2,1)S(1)}, u32[]{:S(2)}, u32[]{:S(2)}) collective-permute-start(bf16[64,512]{1,0:T(8,128)(2,1)S(1)} %get-tuple-element.69), channel_id=1, source_target_pairs={{2,0},{4,2},{6,4},{8,6},{10,8},{12,10},{14,12},{16,14},{18,16},{20... | collective-permute-start | bytes 196616 | tf_op jit(solution)/shard_map/ppermute | solution.py:19
  98.1 9.3 %copy-start.4 = (f32[64,4096]{1,0:T(8,128)}, f32[64,4096]{1,0:T(8,128)S(1)}, u32[]{:S(2)}) copy-start(f32[64,4096]{1,0:T(8,128)S(1)} %add.78) | copy-start | bytes 3145732
  98.1 9.1 %collective-permute-start.10 = (f32[64,1]{1,0:T(8,128)S(1)}, f32[64,1]{1,0:T(8,128)S(1)}, u32[]{:S(2)}, u32[]{:S(2)}) collective-permute-start(f32[64,1]{1,0:T(8,128)S(1)} %get-tuple-element.28), channel_id=1, source_target_pairs={{0,2},{2,4},{4,6},{6,8},{8,10},{10,12},{12,14},{14,16},{16,18},{18... | collective-permute-start | bytes 776 | tf_op jit(solution)/shard_map/ppermute | solution.py:16
  98.2 9.2 %collective-permute-start.11 = (f32[64,1]{1,0:T(8,128)S(1)}, f32[64,1]{1,0:T(8,128)S(1)}, u32[]{:S(2)}, u32[]{:S(2)}) collective-permute-start(f32[64,1]{1,0:T(8,128)S(1)} %get-tuple-element.29), channel_id=1, source_target_pairs={{2,0},{4,2},{6,4},{8,6},{10,8},{12,10},{14,12},{16,14},{18,16},{20... | collective-permute-start | bytes 776 | tf_op jit(solution)/shard_map/ppermute | solution.py:19
  108.0 23.7 %copy-start.5 = (f32[64,4096]{1,0:T(8,128)S(1)}, f32[64,4096]{1,0:T(8,128)}, u32[]{:S(2)}) copy-start(f32[64,4096]{1,0:T(8,128)} %copy-done.4) | copy-start | bytes 3145732
  108.1 9.5 %collective-permute-start.12 = (bf16[64,512]{1,0:T(8,128)(2,1)S(1)}, bf16[64,512]{1,0:T(8,128)(2,1)S(1)}, u32[]{:S(2)}, u32[]{:S(2)}) collective-permute-start(bf16[64,512]{1,0:T(8,128)(2,1)S(1)} %get-tuple-element.62), channel_id=1, source_target_pairs={{0,2},{2,4},{4,6},{6,8},{8,10},{10,12},{12,14},{14,16},{16,18},{18... | collective-permute-start | bytes 196616 | tf_op jit(solution)/shard_map/ppermute | solution.py:16
  108.1 9.4 %collective-permute-start.13 = (bf16[64,512]{1,0:T(8,128)(2,1)S(1)}, bf16[64,512]{1,0:T(8,128)(2,1)S(1)}, u32[]{:S(2)}, u32[]{:S(2)}) collective-permute-start(bf16[64,512]{1,0:T(8,128)(2,1)S(1)} %get-tuple-element.63), channel_id=1, source_target_pairs={{2,0},{4,2},{6,4},{8,6},{10,8},{12,10},{14,12},{16,14},{18,16},{20... | collective-permute-start | bytes 196616 | tf_op jit(solution)/shard_map/ppermute | solution.py:19
  131.9 18.1 %copy-start.7 = (f32[64,4096]{1,0:T(8,128)}, f32[64,4096]{1,0:T(8,128)S(1)}, u32[]{:S(2)}) copy-start(f32[64,4096]{1,0:T(8,128)S(1)} %add.80) | copy-start | bytes 3145732
  132.0 16.4 %collective-permute-start.14 = (f32[64,1]{1,0:T(8,128)S(1)}, f32[64,1]{1,0:T(8,128)S(1)}, u32[]{:S(2)}, u32[]{:S(2)}) collective-permute-start(f32[64,1]{1,0:T(8,128)S(1)} %get-tuple-element.26), channel_id=1, source_target_pairs={{0,2},{2,4},{4,6},{6,8},{8,10},{10,12},{12,14},{14,16},{16,18},{18... | collective-permute-start | bytes 776 | tf_op jit(solution)/shard_map/ppermute | solution.py:16
  132.0 18.0 %collective-permute-start.15 = (f32[64,1]{1,0:T(8,128)S(1)}, f32[64,1]{1,0:T(8,128)S(1)}, u32[]{:S(2)}, u32[]{:S(2)}) collective-permute-start(f32[64,1]{1,0:T(8,128)S(1)} %get-tuple-element.27), channel_id=1, source_target_pairs={{2,0},{4,2},{6,4},{8,6},{10,8},{12,10},{14,12},{16,14},{18,16},{20... | collective-permute-start | bytes 776 | tf_op jit(solution)/shard_map/ppermute | solution.py:19
  257.2 453.1 %reduce-scatter.5.cloned.1.call-start = ((), (), s32[]{:S(2)}) async-start(), calls=%async_computation.5 | async-start | bytes 49152 | tf_op jit(solution)/shard_map/reduce_scatter | solution.py:75
  269.9 9.2 %copy-start.2 = (f32[64,4096]{1,0:T(8,128)}, f32[64,4096]{1,0:T(8,128)S(1)}, u32[]{:S(2)}) copy-start(f32[64,4096]{1,0:T(8,128)S(1)} %add.82) | copy-start | bytes 3145732
  270.0 9.1 %collective-permute-start.16 = (f32[64,1]{1,0:T(8,128)S(1)}, f32[64,1]{1,0:T(8,128)S(1)}, u32[]{:S(2)}, u32[]{:S(2)}) collective-permute-start(f32[64,1]{1,0:T(8,128)S(1)} %get-tuple-element.24), channel_id=1, source_target_pairs={{0,2},{2,4},{4,6},{6,8},{8,10},{10,12},{12,14},{14,16},{16,18},{18... | collective-permute-start | bytes 776 | tf_op jit(solution)/shard_map/ppermute | solution.py:16
  270.0 9.1 %collective-permute-start.17 = (f32[64,1]{1,0:T(8,128)S(1)}, f32[64,1]{1,0:T(8,128)S(1)}, u32[]{:S(2)}, u32[]{:S(2)}) collective-permute-start(f32[64,1]{1,0:T(8,128)S(1)} %get-tuple-element.25), channel_id=1, source_target_pairs={{2,0},{4,2},{6,4},{8,6},{10,8},{12,10},{14,12},{16,14},{18,16},{20... | collective-permute-start | bytes 776 | tf_op jit(solution)/shard_map/ppermute | solution.py:19
  452.5 9.5 %collective-permute-start.18 = (bf16[64,512]{1,0:T(8,128)(2,1)S(1)}, bf16[64,512]{1,0:T(8,128)(2,1)S(1)}, u32[]{:S(2)}, u32[]{:S(2)}) collective-permute-start(bf16[64,512]{1,0:T(8,128)(2,1)S(1)} %get-tuple-element.56), channel_id=1, source_target_pairs={{0,2},{2,4},{4,6},{6,8},{8,10},{10,12},{12,14},{14,16},{16,18},{18... | collective-permute-start | bytes 196616 | tf_op jit(solution)/shard_map/ppermute | solution.py:16
  452.6 9.4 %collective-permute-start.19 = (bf16[64,512]{1,0:T(8,128)(2,1)S(1)}, bf16[64,512]{1,0:T(8,128)(2,1)S(1)}, u32[]{:S(2)}, u32[]{:S(2)}) collective-permute-start(bf16[64,512]{1,0:T(8,128)(2,1)S(1)} %get-tuple-element.57), channel_id=1, source_target_pairs={{2,0},{4,2},{6,4},{8,6},{10,8},{12,10},{14,12},{16,14},{18,16},{20... | collective-permute-start | bytes 196616 | tf_op jit(solution)/shard_map/ppermute | solution.py:19
  475.4 33.9 %copy-start.9 = (f32[4,8,8,1024]{3,2,0,1:T(8,128)}, f32[4,8,8,1024]{3,2,0,1:T(8,128)S(1)}, u32[]{:S(2)}) copy-start(f32[4,8,8,1024]{3,2,0,1:T(8,128)S(1)} %copy.98) | copy-start | bytes 3145732
  475.5 9.1 %collective-permute-start.20 = (f32[64,1]{1,0:T(8,128)S(1)}, f32[64,1]{1,0:T(8,128)S(1)}, u32[]{:S(2)}, u32[]{:S(2)}) collective-permute-start(f32[64,1]{1,0:T(8,128)S(1)} %get-tuple-element.22), channel_id=1, source_target_pairs={{0,2},{2,4},{4,6},{6,8},{8,10},{10,12},{12,14},{14,16},{16,18},{18... | collective-permute-start | bytes 776 | tf_op jit(solution)/shard_map/ppermute | solution.py:16
  475.5 9.1 %collective-permute-start.21 = (f32[64,1]{1,0:T(8,128)S(1)}, f32[64,1]{1,0:T(8,128)S(1)}, u32[]{:S(2)}, u32[]{:S(2)}) collective-permute-start(f32[64,1]{1,0:T(8,128)S(1)} %get-tuple-element.23), channel_id=1, source_target_pairs={{2,0},{4,2},{6,4},{8,6},{10,8},{12,10},{14,12},{16,14},{18,16},{20... | collective-permute-start | bytes 776 | tf_op jit(solution)/shard_map/ppermute | solution.py:19
  485.3 9.5 %collective-permute-start.22 = (bf16[64,512]{1,0:T(8,128)(2,1)S(1)}, bf16[64,512]{1,0:T(8,128)(2,1)S(1)}, u32[]{:S(2)}, u32[]{:S(2)}) collective-permute-start(bf16[64,512]{1,0:T(8,128)(2,1)S(1)} %get-tuple-element.50), channel_id=1, source_target_pairs={{0,2},{2,4},{4,6},{6,8},{8,10},{10,12},{12,14},{14,16},{16,18},{18... | collective-permute-start | bytes 196616 | tf_op jit(solution)/shard_map/ppermute | solution.py:16
  485.4 9.7 %collective-permute-start.23 = (bf16[64,512]{1,0:T(8,128)(2,1)S(1)}, bf16[64,512]{1,0:T(8,128)(2,1)S(1)}, u32[]{:S(2)}, u32[]{:S(2)}) collective-permute-start(bf16[64,512]{1,0:T(8,128)(2,1)S(1)} %get-tuple-element.51), channel_id=1, source_target_pairs={{2,0},{4,2},{6,4},{8,6},{10,8},{12,10},{14,12},{16,14},{18,16},{20... | collective-permute-start | bytes 196616 | tf_op jit(solution)/shard_map/ppermute | solution.py:19
  510.7 9.1 %collective-permute-start.24 = (f32[64,1]{1,0:T(8,128)S(1)}, f32[64,1]{1,0:T(8,128)S(1)}, u32[]{:S(2)}, u32[]{:S(2)}) collective-permute-start(f32[64,1]{1,0:T(8,128)S(1)} %get-tuple-element.20), channel_id=1, source_target_pairs={{0,2},{2,4},{4,6},{6,8},{8,10},{10,12},{12,14},{14,16},{16,18},{18... | collective-permute-start | bytes 776 | tf_op jit(solution)/shard_map/ppermute | solution.py:16
  510.7 9.2 %collective-permute-start.25 = (f32[64,1]{1,0:T(8,128)S(1)}, f32[64,1]{1,0:T(8,128)S(1)}, u32[]{:S(2)}, u32[]{:S(2)}) collective-permute-start(f32[64,1]{1,0:T(8,128)S(1)} %get-tuple-element.21), channel_id=1, source_target_pairs={{2,0},{4,2},{6,4},{8,6},{10,8},{12,10},{14,12},{16,14},{18,16},{20... | collective-permute-start | bytes 776 | tf_op jit(solution)/shard_map/ppermute | solution.py:19
  520.6 9.5 %collective-permute-start.26 = (bf16[64,512]{1,0:T(8,128)(2,1)S(1)}, bf16[64,512]{1,0:T(8,128)(2,1)S(1)}, u32[]{:S(2)}, u32[]{:S(2)}) collective-permute-start(bf16[64,512]{1,0:T(8,128)(2,1)S(1)} %get-tuple-element.44), channel_id=1, source_target_pairs={{0,2},{2,4},{4,6},{6,8},{8,10},{10,12},{12,14},{14,16},{16,18},{18... | collective-permute-start | bytes 196616 | tf_op jit(solution)/shard_map/ppermute | solution.py:16
  520.7 9.4 %collective-permute-start.27 = (bf16[64,512]{1,0:T(8,128)(2,1)S(1)}, bf16[64,512]{1,0:T(8,128)(2,1)S(1)}, u32[]{:S(2)}, u32[]{:S(2)}) collective-permute-start(bf16[64,512]{1,0:T(8,128)(2,1)S(1)} %get-tuple-element.45), channel_id=1, source_target_pairs={{2,0},{4,2},{6,4},{8,6},{10,8},{12,10},{14,12},{16,14},{18,16},{20... | collective-permute-start | bytes 196616 | tf_op jit(solution)/shard_map/ppermute | solution.py:19
  544.4 9.3 %copy-start.6 = (f32[64,4096]{1,0:T(8,128)}, f32[64,4096]{1,0:T(8,128)S(1)}, u32[]{:S(2)}) copy-start(f32[64,4096]{1,0:T(8,128)S(1)} %add.88) | copy-start | bytes 3145732
  544.5 9.1 %collective-permute-start.28 = (f32[64,1]{1,0:T(8,128)S(1)}, f32[64,1]{1,0:T(8,128)S(1)}, u32[]{:S(2)}, u32[]{:S(2)}) collective-permute-start(f32[64,1]{1,0:T(8,128)S(1)} %get-tuple-element.18), channel_id=1, source_target_pairs={{0,2},{2,4},{4,6},{6,8},{8,10},{10,12},{12,14},{14,16},{16,18},{18... | collective-permute-start | bytes 776 | tf_op jit(solution)/shard_map/ppermute | solution.py:16
  544.5 9.2 %collective-permute-start.29 = (f32[64,1]{1,0:T(8,128)S(1)}, f32[64,1]{1,0:T(8,128)S(1)}, u32[]{:S(2)}, u32[]{:S(2)}) collective-permute-start(f32[64,1]{1,0:T(8,128)S(1)} %get-tuple-element.19), channel_id=1, source_target_pairs={{2,0},{4,2},{6,4},{8,6},{10,8},{12,10},{14,12},{16,14},{18,16},{20... | collective-permute-start | bytes 776 | tf_op jit(solution)/shard_map/ppermute | solution.py:19
  554.4 9.5 %collective-permute-start.30 = (bf16[64,512]{1,0:T(8,128)(2,1)S(1)}, bf16[64,512]{1,0:T(8,128)(2,1)S(1)}, u32[]{:S(2)}, u32[]{:S(2)}) collective-permute-start(bf16[64,512]{1,0:T(8,128)(2,1)S(1)} %get-tuple-element.38), channel_id=1, source_target_pairs={{0,2},{2,4},{4,6},{6,8},{8,10},{10,12},{12,14},{14,16},{16,18},{18... | collective-permute-start | bytes 196616 | tf_op jit(solution)/shard_map/ppermute | solution.py:16
  554.5 9.7 %collective-permute-start.31 = (bf16[64,512]{1,0:T(8,128)(2,1)S(1)}, bf16[64,512]{1,0:T(8,128)(2,1)S(1)}, u32[]{:S(2)}, u32[]{:S(2)}) collective-permute-start(bf16[64,512]{1,0:T(8,128)(2,1)S(1)} %get-tuple-element.39), channel_id=1, source_target_pairs={{2,0},{4,2},{6,4},{8,6},{10,8},{12,10},{14,12},{16,14},{18,16},{20... | collective-permute-start | bytes 196616 | tf_op jit(solution)/shard_map/ppermute | solution.py:19
  564.3 24.7 %copy-start.14 = (bf16[4,16,1024]{2,1,0:T(8,128)(2,1)S(1)}, bf16[4,16,1024]{2,1,0:T(8,128)(2,1)}, u32[]{:S(2)}) copy-start(bf16[4,16,1024]{2,1,0:T(8,128)(2,1)} %param.10) | copy-start | bytes 393220
  576.3 316.5 %copy-start.3 = (f32[64,4096]{1,0:T(8,128)S(1)}, f32[64,4096]{1,0:T(8,128)}, u32[]{:S(2)}) copy-start(f32[64,4096]{1,0:T(8,128)} %copy-done.2) | copy-start | bytes 3145732
  579.0 9.3 %copy-start.8 = (f32[64,4096]{1,0:T(8,128)}, f32[64,4096]{1,0:T(8,128)S(1)}, u32[]{:S(2)}) copy-start(f32[64,4096]{1,0:T(8,128)S(1)} %add.90) | copy-start | bytes 3145732
  579.1 9.1 %collective-permute-start.32 = (f32[64,1]{1,0:T(8,128)S(1)}, f32[64,1]{1,0:T(8,128)S(1)}, u32[]{:S(2)}, u32[]{:S(2)}) collective-permute-start(f32[64,1]{1,0:T(8,128)S(1)} %get-tuple-element.16), channel_id=1, source_target_pairs={{0,2},{2,4},{4,6},{6,8},{8,10},{10,12},{12,14},{14,16},{16,18},{18... | collective-permute-start | bytes 776 | tf_op jit(solution)/shard_map/ppermute | solution.py:16
  579.2 9.2 %collective-permute-start.33 = (f32[64,1]{1,0:T(8,128)S(1)}, f32[64,1]{1,0:T(8,128)S(1)}, u32[]{:S(2)}, u32[]{:S(2)}) collective-permute-start(f32[64,1]{1,0:T(8,128)S(1)} %get-tuple-element.17), channel_id=1, source_target_pairs={{2,0},{4,2},{6,4},{8,6},{10,8},{12,10},{14,12},{16,14},{18,16},{20... | collective-permute-start | bytes 776 | tf_op jit(solution)/shard_map/ppermute | solution.py:19
  712.9 9.2 %copy-start.11 = (f32[64,4096]{1,0:T(8,128)}, f32[64,4096]{1,0:T(8,128)S(1)}, u32[]{:S(2)}) copy-start(f32[64,4096]{1,0:T(8,128)S(1)} %add.92) | copy-start | bytes 3145732
  713.0 9.1 %collective-permute-start.34 = (f32[64,1]{1,0:T(8,128)S(1)}, f32[64,1]{1,0:T(8,128)S(1)}, u32[]{:S(2)}, u32[]{:S(2)}) collective-permute-start(f32[64,1]{1,0:T(8,128)S(1)} %get-tuple-element.14), channel_id=1, source_target_pairs={{0,2},{2,4},{4,6},{6,8},{8,10},{10,12},{12,14},{14,16},{16,18},{18... | collective-permute-start | bytes 776 | tf_op jit(solution)/shard_map/ppermute | solution.py:16
  713.0 9.1 %collective-permute-start.35 = (f32[64,1]{1,0:T(8,128)S(1)}, f32[64,1]{1,0:T(8,128)S(1)}, u32[]{:S(2)}, u32[]{:S(2)}) collective-permute-start(f32[64,1]{1,0:T(8,128)S(1)} %get-tuple-element.15), channel_id=1, source_target_pairs={{2,0},{4,2},{6,4},{8,6},{10,8},{12,10},{14,12},{16,14},{18,16},{20... | collective-permute-start | bytes 776 | tf_op jit(solution)/shard_map/ppermute | solution.py:19
Sparse Core Ops, SparseCore 0:
  257.3 9.0 reduce-scatter.2
  701.2 9.0 reduce-scatter.4
where the time goes:
time: 913 us; the launch traced here: 904 us
  blocking collectives  553 us (61%)
  starting transfers between devices  147 us (16%)
  matrix products  99.6 us (11%)
  waiting for transfers between devices  49.7 us (5%)
  other arithmetic  27.1 us (3%)
  between operations  15.1 us (2%)
  local copies, waits for them, and re-layouts  12.7 us (1%)
    psum x2, blocking collectives, body(): lax.psum((jnp.sum(residual * image, axis=1), jnp.sum(image * image, axis=...  340 us
    all_gather x2, blocking collectives, body(): gathered = lax.all_gather(projected, 'sector', axis=1, tiled=True)  190 us
    ppermute x18, starting transfers between devices, extended_2(): lax.ppermute(lax.slice_in_dim(block, 0, width, axis=dim), axis, backward)  146 us
    dot_general x8, matrix products, correct(): jnp.einsum('jco,jko->cjk', windows, local_inverse, preferred_element_type...  94.2 us
    ppermute x18, waiting for transfers between devices, extended_2(): lax.ppermute(lax.slice_in_dim(block, block.shape[dim] - width, None, axis...  28.2 us
    all_to_all x2, blocking collectives, body(): lax.all_to_all(gathered.astype(jnp.bfloat16), 'lift', split_axis=1, conca...  22.3 us
    reduce_scatter x2, waiting for transfers between devices, body(): lax.psum_scatter(jnp.dot(swapped, coarse_inverse.T, precision=highest).as...  18.4 us
  transfers between devices with their start and end apart: 38, of which 29 were waited for; matrix products, arithmetic and copies ran while one was open for 0% of the time, Pallas kernels for 0%

commit v1 on v0

--- a/solution.py
+++ b/solution.py
@@ -68,7 +68,10 @@
             coarse_basis,
             preferred_element_type=jnp.float32,
         ).reshape(num_cases, sub_count * mode_count)
-        gathered = lax.all_gather(projected, "sector", axis=1, tiled=True)
+        n_dev = lax.axis_size("sector")
+        pieces = jnp.stack([projected for _ in range(n_dev)])
+        pieces = lax.all_to_all(pieces, "sector", split_axis=0, concat_axis=0)
+        gathered = jnp.concatenate(pieces, axis=1)
         swapped = lax.all_to_all(
             gathered.astype(jnp.bfloat16), "lift", split_axis=1, concat_axis=0, tiled=True
         ).astype(gathered.dtype)

time: 913 us -> 778 us (0.85)
  blocking collectives: 553 us -> 410 us
  local copies, waits for them, and re-layouts: 12.7 us -> 33.8 us
    all_gather x2 -> x0, blocking collectives: 190 us -> none  [body(): gathered = lax.all_gather(projected, 'sector', axis=1, tiled=True)]
    all_to_all x0 -> x2, blocking collectives: none -> 47.9 us  [body(): pieces = lax.all_to_all(pieces, 'sector', split_axis=0, concat_axis=0)]
    convert_element_type x0 -> x6, local copies, waits for them, and re-layouts: none -> 10.8 us  [body(): gathered.astype(jnp.bfloat16)]
    unnamed x30 -> x32, local copies, waits for them, and re-layouts: 0.09 us -> 10.8 us
  transfers between devices with their start and end apart: 38 -> 38, of which waited for: 29 -> 30; matrix products, arithmetic and copies ran while one was open for 0% -> 0% of each run, Pallas kernels for 0% -> 0%
where the time goes in v1:
time: 778 us; the launch traced here: 769 us
  blocking collectives  410 us (53%)
  starting transfers between devices  139 us (18%)
  matrix products  97.7 us (13%)
  waiting for transfers between devices  46.4 us (6%)
  local copies, waits for them, and re-layouts  33.8 us (4%)
  other arithmetic  27.1 us (3%)
  between operations  15.1 us (2%)
    psum x2, blocking collectives, body(): lax.psum((jnp.sum(residual * image, axis=1), jnp.sum(image * image, axis=...  340 us
    ppermute x18, starting transfers between devices, extended_2(): lax.ppermute(lax.slice_in_dim(block, 0, width, axis=dim), axis, backward)  138 us
    dot_general x8, matrix products, correct(): jnp.einsum('jco,jko->cjk', windows, local_inverse, preferred_element_type...  93.2 us
    all_to_all x2, blocking collectives, body(): pieces = lax.all_to_all(pieces, 'sector', split_axis=0, concat_axis=0)  47.9 us
    ppermute x18, waiting for transfers between devices, extended_2(): lax.ppermute(lax.slice_in_dim(block, block.shape[dim] - width, None, axis...  29.2 us
    all_to_all x2, blocking collectives, body(): lax.all_to_all(gathered.astype(jnp.bfloat16), 'lift', split_axis=1, conca...  21.7 us
  transfers between devices with their start and end apart: 38, of which 30 were waited for; matrix products, arithmetic and copies ran while one was open for 0% of the time, Pallas kernels for 0%

profile of v1, /device:TPU:0, one launch (start us, length us, event | category | flops | bytes accessed | tf_op | source)
XLA Modules:
  0.0 768.5 jit_solution(11535195378229328090)
XLA Ops:
  7.3 1.4 convert_element_type.61
  8.7 8.6 %collective-permute-start.1 = (bf16[64,512]{1,0:T(8,128)(2,1)S(1)}, bf16[64,512]{1,0:T(8,128)(2,1)S(1)}, u32[]{:S(2)}, u32[]{:S(2)}) collective-permute-start(bf16[64,512]{1,0:T(8,128)(2,1)S(1)} %get-tuple-element.81), channel_id=1, source_target_pairs={{2,0},{4,2},{6,4},{8,6},{10,8},{12,10},{14,12},{16,14},{18,16},{20... | collective-permute-start | bytes 196616 | tf_op jit(solution)/shard_map/ppermute | solution.py:19
  17.3 1.9 collective-permute-done
  20.0 11.0 %convolution_bitcast_fusion.9 = f32[4,8,8,1024]{3,2,1,0:T(8,128)S(1)} fusion(bf16[4,1024,2048]{2,1,0:T(8,128)(2,1)} %param.9, bf16[1,64,2048]{2,1,0:T(8,128)(2,1)} %get-tuple-element.79, bf16[1,64,2048]{2,1,0:T(8,128)(2,1)S(1)} %get-tuple-element.77, bf16[1,64,2048]{2,1,0:T(8,128)(2,1)S(1)} %get-tuple-element.78, bf16[1,64,2048]{2,1,0:T(8,128)(2,1)S(1)} %get-tuple-element.76), kind=kOutput, calls=%fused_computation.9 | convolution fusion | flops 1075314688 | bytes 18874368 | tf_op jit(solution)/shard_map/jco,jko->cjk/dot_general | solution.py:52
  31.3 7.6 collective-permute-start.3
  38.9 1.5 collective-permute-done.2
  41.3 7.5 collective-permute-start.5
  48.8 1.9 collective-permute-done.4
  51.5 11.1 %convolution_bitcast_fusion.8 = f32[4,8,8,1024]{3,2,1,0:T(8,128)S(1)} fusion(bf16[4,1024,2048]{2,1,0:T(8,128)(2,1)} %param.9, bf16[1,64,2048]{2,1,0:T(8,128)(2,1)} %get-tuple-element.73, bf16[1,64,2048]{2,1,0:T(8,128)(2,1)S(1)} %get-tuple-element.71, bf16[1,64,2048]{2,1,0:T(8,128)(2,1)S(1)} %get-tuple-element.72, bf16[1,64,2048]{2,1,0:T(8,128)(2,1)S(1)} %get-tuple-element.70), kind=kOutput, calls=%fused_computation.8 | convolution fusion | flops 1075314688 | bytes 18874368 | tf_op jit(solution)/shard_map/jco,jko->cjk/dot_general | solution.py:52
  62.7 1.3 add.76
  64.1 7.8 %collective-permute-start.7 = (f32[64,1]{1,0:T(8,128)S(1)}, f32[64,1]{1,0:T(8,128)S(1)}, u32[]{:S(2)}, u32[]{:S(2)}) collective-permute-start(f32[64,1]{1,0:T(8,128)S(1)} %get-tuple-element.31), channel_id=1, source_target_pairs={{2,0},{4,2},{6,4},{8,6},{10,8},{12,10},{14,12},{16,14},{18,16},{20... | collective-permute-start | bytes 776 | tf_op jit(solution)/shard_map/ppermute | solution.py:19
  74.3 7.5 collective-permute-start.9
  81.8 1.9 collective-permute-done.8
  84.6 12.0 %convolution_bitcast_fusion.7 = f32[4,8,8,1024]{3,2,1,0:T(8,128)} fusion(bf16[4,1024,2048]{2,1,0:T(8,128)(2,1)} %param.9, bf16[1,64,2048]{2,1,0:T(8,128)(2,1)} %get-tuple-element.67, bf16[1,64,2048]{2,1,0:T(8,128)(2,1)S(1)} %get-tuple-element.65, bf16[1,64,2048]{2,1,0:T(8,128)(2,1)S(1)} %get-tuple-element.66, bf16[1,64,2048]{2,1,0:T(8,128)(2,1)S(1)} %get-tuple-element.64), kind=kOutput, calls=%fused_computation.7 | convolution fusion | flops 1075314688 | bytes 18874368 | tf_op jit(solution)/shard_map/jco,jko->cjk/dot_general | solution.py:52
  98.1 7.6 collective-permute-start.11
  105.7 1.5 collective-permute-done.10
  108.1 7.5 collective-permute-start.13
  115.6 1.9 collective-permute-done.12
  118.4 11.0 %convolution_bitcast_fusion.6 = f32[4,8,8,1024]{3,2,1,0:T(8,128)S(1)} fusion(bf16[4,1024,2048]{2,1,0:T(8,128)(2,1)} %param.9, bf16[1,64,2048]{2,1,0:T(8,128)(2,1)} %get-tuple-element.61, bf16[1,64,2048]{2,1,0:T(8,128)(2,1)S(1)} %get-tuple-element.59, bf16[1,64,2048]{2,1,0:T(8,128)(2,1)S(1)} %get-tuple-element.60, bf16[1,64,2048]{2,1,0:T(8,128)(2,1)S(1)} %get-tuple-element.58), kind=kOutput, calls=%fused_computation.6 | convolution fusion | flops 1075314688 | bytes 18874368 | tf_op jit(solution)/shard_map/jco,jko->cjk/dot_general | solution.py:52
  129.5 1.3 add.80
  131.0 8.0 %collective-permute-start.15 = (f32[64,1]{1,0:T(8,128)S(1)}, f32[64,1]{1,0:T(8,128)S(1)}, u32[]{:S(2)}, u32[]{:S(2)}) collective-permute-start(f32[64,1]{1,0:T(8,128)S(1)} %get-tuple-element.27), channel_id=1, source_target_pairs={{2,0},{4,2},{6,4},{8,6},{10,8},{12,10},{14,12},{16,14},{18,16},{20... | collective-permute-start | bytes 776 | tf_op jit(solution)/shard_map/ppermute | solution.py:19
  143.7 2.3 reshape.82
  146.1 23.9 %all_to_all.42 = bf16[64,2,2048]{2,1,0:T(2,128)(2,1)} all-to-all(bf16[64,2,2048]{2,1,0:T(2,128)(2,1)S(1)} %reshape.82), channel_id=1, replica_groups=mesh['sector'=64,'lift'=2] {'sector'}, dimensions={0} | all-to-all | bytes 1048576 | tf_op jit(solution)/shard_map/all_to_all | solution.py:73
  170.0 3.0 reshape.83
  173.0 2.9 copy.47
  175.9 2.3 convert_element_type.68
  178.4 10.9 %all_to_all.43 = bf16[64,2,2048]{2,0,1:T(8,128)(2,1)S(1)} all-to-all(bf16[64,2,2048]{2,0,1:T(8,128)(2,1)S(1)} %copy.48), channel_id=1, replica_groups=mesh['sector'=64,'lift'=2] {'lift'}, dimensions={1} | all-to-all | bytes 1048576 | tf_op jit(solution)/shard_map/all_to_all | solution.py:75
  190.6 7.6 reduce-scatter.3.cloned.1.call-done
  199.6 7.5 collective-permute-start.17
  207.1 1.6 collective-permute-done.16
  209.5 170.0 %all-reduce.1 = (f32[64]{0:T(128)S(1)}, f32[64]{0:T(128)S(1)}) all-reduce(f32[64]{0:T(128)S(1)} %get-tuple-element.5, f32[64]{0:T(128)S(1)} %get-tuple-element.4), channel_id=1, replica_groups=mesh['sector'=64,'lift'=2] {'sector'}, use_global_device_ids=true, to_apply=%region_2.0 | all-reduce | flops 128 | bytes 1024 | tf_op jit(solution)/shard_map/psum | solution.py:89
  379.4 2.6 fusion.132
  382.1 7.6 collective-permute-start.19
  389.7 1.8 collective-permute-done.18
  391.8 11.9 %convolution_bitcast_fusion.4 = f32[4,8,8,1024]{3,2,1,0:T(8,128)} fusion(bf16[4,1024,2048]{2,1,0:T(8,128)(2,1)} %param.9, bf16[1,64,2048]{2,1,0:T(8,128)(2,1)S(1)} %get-tuple-element.55, bf16[1,64,2048]{2,1,0:T(8,128)(2,1)S(1)} %get-tuple-element.53, bf16[1,64,2048]{2,1,0:T(8,128)(2,1)S(1)} %get-tuple-element.54, bf16[1,64,2048]{2,1,0:T(8,128)(2,1)S(1)} %get-tuple-element.52), kind=kOutput, calls=%fused_computation.4 | convolution fusion | flops 1075314688 | bytes 18874368 | tf_op jit(solution)/shard_map/jco,jko->cjk/dot_general | solution.py:52
  405.1 7.6 collective-permute-start.21
  412.7 1.5 collective-permute-done.20
  415.1 7.5 collective-permute-start.23
  422.6 1.9 collective-permute-done.22
  425.4 12.1 %convolution_bitcast_fusion.3 = f32[4,8,8,1024]{3,2,1,0:T(8,128)} fusion(bf16[4,1024,2048]{2,1,0:T(8,128)(2,1)} %param.9, bf16[1,64,2048]{2,1,0:T(8,128)(2,1)} %get-tuple-element.49, bf16[1,64,2048]{2,1,0:T(8,128)(2,1)S(1)} %get-tuple-element.47, bf16[1,64,2048]{2,1,0:T(8,128)(2,1)S(1)} %get-tuple-element.48, bf16[1,64,2048]{2,1,0:T(8,128)(2,1)S(1)} %get-tuple-element.46), kind=kOutput, calls=%fused_computation.3 | convolution fusion | flops 1075314688 | bytes 18874368 | tf_op jit(solution)/shard_map/jco,jko->cjk/dot_general | solution.py:52
  438.8 1.3 add.86
  440.2 7.6 collective-permute-start.25
  447.8 1.5 collective-permute-done.24
  450.2 7.7 %collective-permute-start.27 = (bf16[64,512]{1,0:T(8,128)(2,1)S(1)}, bf16[64,512]{1,0:T(8,128)(2,1)S(1)}, u32[]{:S(2)}, u32[]{:S(2)}) collective-permute-start(bf16[64,512]{1,0:T(8,128)(2,1)S(1)} %get-tuple-element.45), channel_id=1, source_target_pairs={{2,0},{4,2},{6,4},{8,6},{10,8},{12,10},{14,12},{16,14},{18,16},{20... | collective-permute-start | bytes 196616 | tf_op jit(solution)/shard_map/ppermute | solution.py:19
  457.9 1.7 collective-permute-done.26
  460.6 12.0 %convolution_bitcast_fusion.2 = f32[4,8,8,1024]{3,2,1,0:T(8,128)} fusion(bf16[4,1024,2048]{2,1,0:T(8,128)(2,1)} %param.9, bf16[1,64,2048]{2,1,0:T(8,128)(2,1)} %get-tuple-element.43, bf16[1,64,2048]{2,1,0:T(8,128)(2,1)S(1)} %get-tuple-element.41, bf16[1,64,2048]{2,1,0:T(8,128)(2,1)S(1)} %get-tuple-element.42, bf16[1,64,2048]{2,1,0:T(8,128)(2,1)S(1)} %get-tuple-element.40), kind=kOutput, calls=%fused_computation.2 | convolution fusion | flops 1075314688 | bytes 18874368 | tf_op jit(solution)/shard_map/jco,jko->cjk/dot_general | solution.py:52
  474.2 7.6 collective-permute-start.29
  481.8 1.5 collective-permute-done.28
  484.2 7.5 collective-permute-start.31
  491.7 1.9 collective-permute-done.30
  493.7 12.0 %convolution_bitcast_fusion.1 = f32[4,8,8,1024]{3,2,1,0:T(8,128)} fusion(bf16[4,1024,2048]{2,1,0:T(8,128)(2,1)} %param.9, bf16[1,64,2048]{2,1,0:T(8,128)(2,1)S(1)} %get-tuple-element.37, bf16[1,64,2048]{2,1,0:T(8,128)(2,1)S(1)} %get-tuple-element.35, bf16[1,64,2048]{2,1,0:T(8,128)(2,1)S(1)} %get-tuple-element.36, bf16[1,64,2048]{2,1,0:T(8,128)(2,1)S(1)} %get-tuple-element.34), kind=kOutput, calls=%fused_computation.1 | convolution fusion | flops 1075314688 | bytes 18874368 | tf_op jit(solution)/shard_map/jco,jko->cjk/dot_general | solution.py:52
  505.8 1.4 copy.71
  508.6 7.8 %collective-permute-start.33 = (f32[64,1]{1,0:T(8,128)S(1)}, f32[64,1]{1,0:T(8,128)S(1)}, u32[]{:S(2)}, u32[]{:S(2)}) collective-permute-start(f32[64,1]{1,0:T(8,128)S(1)} %get-tuple-element.17), channel_id=1, source_target_pairs={{2,0},{4,2},{6,4},{8,6},{10,8},{12,10},{14,12},{16,14},{18,16},{20... | collective-permute-start | bytes 776 | tf_op jit(solution)/shard_map/ppermute | solution.py:19
  520.4 2.3 reshape.84
  522.7 23.9 %all_to_all.44 = bf16[64,2,2048]{2,1,0:T(2,128)(2,1)} all-to-all(bf16[64,2,2048]{2,1,0:T(2,128)(2,1)S(1)} %reshape.84), channel_id=1, replica_groups=mesh['sector'=64,'lift'=2] {'sector'}, dimensions={0} | all-to-all | bytes 1048576 | tf_op jit(solution)/shard_map/all_to_all | solution.py:73
  546.7 3.0 reshape.85
  549.7 2.9 copy.57
  552.6 2.3 convert_element_type.77
  555.1 10.9 %all_to_all.45 = bf16[64,2,2048]{2,0,1:T(8,128)(2,1)S(1)} all-to-all(bf16[64,2,2048]{2,0,1:T(8,128)(2,1)S(1)} %copy.58), channel_id=1, replica_groups=mesh['sector'=64,'lift'=2] {'lift'}, dimensions={1} | all-to-all | bytes 1048576 | tf_op jit(solution)/shard_map/all_to_all | solution.py:75
  567.2 7.6 reduce-scatter.5.cloned.1.call-done
  577.5 7.5 collective-permute-start.35
  585.0 1.6 collective-permute-done.34
  587.4 170.0 %all-reduce = (f32[64]{0:T(128)S(1)}, f32[64]{0:T(128)S(1)}) all-reduce(f32[64]{0:T(128)S(1)} %get-tuple-element.3, f32[64]{0:T(128)S(1)} %get-tuple-element.2), channel_id=1, replica_groups=mesh['sector'=64,'lift'=2] {'sector'}, use_global_device_ids=true, to_apply=%region_7.0 | all-reduce | flops 128 | bytes 1024 | tf_op jit(solution)/shard_map/psum | solution.py:89
  757.4 3.9 multiply_subtract_fusion
  (137 shorter events, 37.5 us)
Async XLA Ops:
  7.2 182.1 %copy-start = (f32[64,2048]{1,0:T(8,128)S(1)}, f32[64,2048]{1,0:T(8,128)}, u32[]{:S(2)}) copy-start(f32[64,2048]{1,0:T(8,128)} %param.11) | copy-start | bytes 1572868
  7.2 33.3 %copy-start.1 = (f32[64,4096]{1,0:T(8,128)S(1)}, f32[64,4096]{1,0:T(8,128)}, u32[]{:S(2)}) copy-start(f32[64,4096]{1,0:T(8,128)} %param.6) | copy-start | bytes 3145732
  7.2 33.3 %copy-start.10 = (f32[4096]{0:T(1024)S(1)}, f32[4096]{0:T(1024)}, u32[]{:S(2)}) copy-start(f32[4096]{0:T(1024)} %param.8) | copy-start | bytes 49156
  7.2 33.3 %copy-start.11 = (f32[4096]{0:T(1024)S(1)}, f32[4096]{0:T(1024)}, u32[]{:S(2)}) copy-start(f32[4096]{0:T(1024)} %param.7) | copy-start | bytes 49156
  7.2 190.9 %reduce-scatter.3.cloned.1.call-start = ((), (), s32[]{:S(2)}) async-start(), calls=%async_computation.6 | async-start | bytes 49152 | tf_op jit(solution)/shard_map/reduce_scatter | solution.py:78
  8.7 10.5 %collective-permute-start = (bf16[64,512]{1,0:T(8,128)(2,1)S(1)}, bf16[64,512]{1,0:T(8,128)(2,1)S(1)}, u32[]{:S(2)}, u32[]{:S(2)}) collective-permute-start(bf16[64,512]{1,0:T(8,128)(2,1)S(1)} %get-tuple-element.80), channel_id=1, source_target_pairs={{0,2},{2,4},{4,6},{6,8},{8,10},{10,12},{12,14},{14,16},{16,18},{18... | collective-permute-start | bytes 196616 | tf_op jit(solution)/shard_map/ppermute | solution.py:16
  8.7 10.5 %collective-permute-start.1 = (bf16[64,512]{1,0:T(8,128)(2,1)S(1)}, bf16[64,512]{1,0:T(8,128)(2,1)S(1)}, u32[]{:S(2)}, u32[]{:S(2)}) collective-permute-start(bf16[64,512]{1,0:T(8,128)(2,1)S(1)} %get-tuple-element.81), channel_id=1, source_target_pairs={{2,0},{4,2},{6,4},{8,6},{10,8},{12,10},{14,12},{16,14},{18,16},{20... | collective-permute-start | bytes 196616 | tf_op jit(solution)/shard_map/ppermute | solution.py:19
  31.2 9.3 %copy-start.8 = (f32[4,8,8,1024]{3,2,0,1:T(8,128)}, f32[4,8,8,1024]{3,2,0,1:T(8,128)S(1)}, u32[]{:S(2)}) copy-start(f32[4,8,8,1024]{3,2,0,1:T(8,128)S(1)} %copy.63) | copy-start | bytes 3145732
  31.3 9.1 %collective-permute-start.2 = (f32[64,1]{1,0:T(8,128)S(1)}, f32[64,1]{1,0:T(8,128)S(1)}, u32[]{:S(2)}, u32[]{:S(2)}) collective-permute-start(f32[64,1]{1,0:T(8,128)S(1)} %get-tuple-element.32), channel_id=1, source_target_pairs={{0,2},{2,4},{4,6},{6,8},{8,10},{10,12},{12,14},{14,16},{16,18},{18... | collective-permute-start | bytes 776 | tf_op jit(solution)/shard_map/ppermute | solution.py:16
  31.3 9.2 %collective-permute-start.3 = (f32[64,1]{1,0:T(8,128)S(1)}, f32[64,1]{1,0:T(8,128)S(1)}, u32[]{:S(2)}, u32[]{:S(2)}) collective-permute-start(f32[64,1]{1,0:T(8,128)S(1)} %get-tuple-element.33), channel_id=1, source_target_pairs={{2,0},{4,2},{6,4},{8,6},{10,8},{12,10},{14,12},{16,14},{18,16},{20... | collective-permute-start | bytes 776 | tf_op jit(solution)/shard_map/ppermute | solution.py:19
  41.2 9.5 %collective-permute-start.4 = (bf16[64,512]{1,0:T(8,128)(2,1)S(1)}, bf16[64,512]{1,0:T(8,128)(2,1)S(1)}, u32[]{:S(2)}, u32[]{:S(2)}) collective-permute-start(bf16[64,512]{1,0:T(8,128)(2,1)S(1)} %get-tuple-element.74), channel_id=1, source_target_pairs={{0,2},{2,4},{4,6},{6,8},{8,10},{10,12},{12,14},{14,16},{16,18},{18... | collective-permute-start | bytes 196616 | tf_op jit(solution)/shard_map/ppermute | solution.py:16
  41.3 9.4 %collective-permute-start.5 = (bf16[64,512]{1,0:T(8,128)(2,1)S(1)}, bf16[64,512]{1,0:T(8,128)(2,1)S(1)}, u32[]{:S(2)}, u32[]{:S(2)}) collective-permute-start(bf16[64,512]{1,0:T(8,128)(2,1)S(1)} %get-tuple-element.75), channel_id=1, source_target_pairs={{2,0},{4,2},{6,4},{8,6},{10,8},{12,10},{14,12},{16,14},{18,16},{20... | collective-permute-start | bytes 196616 | tf_op jit(solution)/shard_map/ppermute | solution.py:19
  64.1 9.1 %collective-permute-start.6 = (f32[64,1]{1,0:T(8,128)S(1)}, f32[64,1]{1,0:T(8,128)S(1)}, u32[]{:S(2)}, u32[]{:S(2)}) collective-permute-start(f32[64,1]{1,0:T(8,128)S(1)} %get-tuple-element.30), channel_id=1, source_target_pairs={{0,2},{2,4},{4,6},{6,8},{8,10},{10,12},{12,14},{14,16},{16,18},{18... | collective-permute-start | bytes 776 | tf_op jit(solution)/shard_map/ppermute | solution.py:16
  64.1 9.4 %collective-permute-start.7 = (f32[64,1]{1,0:T(8,128)S(1)}, f32[64,1]{1,0:T(8,128)S(1)}, u32[]{:S(2)}, u32[]{:S(2)}) collective-permute-start(f32[64,1]{1,0:T(8,128)S(1)} %get-tuple-element.31), channel_id=1, source_target_pairs={{2,0},{4,2},{6,4},{8,6},{10,8},{12,10},{14,12},{16,14},{18,16},{20... | collective-permute-start | bytes 776 | tf_op jit(solution)/shard_map/ppermute | solution.py:19
  74.2 9.5 %collective-permute-start.8 = (bf16[64,512]{1,0:T(8,128)(2,1)S(1)}, bf16[64,512]{1,0:T(8,128)(2,1)S(1)}, u32[]{:S(2)}, u32[]{:S(2)}) collective-permute-start(bf16[64,512]{1,0:T(8,128)(2,1)S(1)} %get-tuple-element.68), channel_id=1, source_target_pairs={{0,2},{2,4},{4,6},{6,8},{8,10},{10,12},{12,14},{14,16},{16,18},{18... | collective-permute-start | bytes 196616 | tf_op jit(solution)/shard_map/ppermute | solution.py:16
  74.3 9.4 %collective-permute-start.9 = (bf16[64,512]{1,0:T(8,128)(2,1)S(1)}, bf16[64,512]{1,0:T(8,128)(2,1)S(1)}, u32[]{:S(2)}, u32[]{:S(2)}) collective-permute-start(bf16[64,512]{1,0:T(8,128)(2,1)S(1)} %get-tuple-element.69), channel_id=1, source_target_pairs={{2,0},{4,2},{6,4},{8,6},{10,8},{12,10},{14,12},{16,14},{18,16},{20... | collective-permute-start | bytes 196616 | tf_op jit(solution)/shard_map/ppermute | solution.py:19
  98.0 9.3 %copy-start.5 = (f32[64,4096]{1,0:T(8,128)}, f32[64,4096]{1,0:T(8,128)S(1)}, u32[]{:S(2)}) copy-start(f32[64,4096]{1,0:T(8,128)S(1)} %add.78) | copy-start | bytes 3145732
  98.1 9.1 %collective-permute-start.10 = (f32[64,1]{1,0:T(8,128)S(1)}, f32[64,1]{1,0:T(8,128)S(1)}, u32[]{:S(2)}, u32[]{:S(2)}) collective-permute-start(f32[64,1]{1,0:T(8,128)S(1)} %get-tuple-element.28), channel_id=1, source_target_pairs={{0,2},{2,4},{4,6},{6,8},{8,10},{10,12},{12,14},{14,16},{16,18},{18... | collective-permute-start | bytes 776 | tf_op jit(solution)/shard_map/ppermute | solution.py:16
  98.1 9.2 %collective-permute-start.11 = (f32[64,1]{1,0:T(8,128)S(1)}, f32[64,1]{1,0:T(8,128)S(1)}, u32[]{:S(2)}, u32[]{:S(2)}) collective-permute-start(f32[64,1]{1,0:T(8,128)S(1)} %get-tuple-element.29), channel_id=1, source_target_pairs={{2,0},{4,2},{6,4},{8,6},{10,8},{12,10},{14,12},{16,14},{18,16},{20... | collective-permute-start | bytes 776 | tf_op jit(solution)/shard_map/ppermute | solution.py:19
  108.0 9.5 %collective-permute-start.12 = (bf16[64,512]{1,0:T(8,128)(2,1)S(1)}, bf16[64,512]{1,0:T(8,128)(2,1)S(1)}, u32[]{:S(2)}, u32[]{:S(2)}) collective-permute-start(bf16[64,512]{1,0:T(8,128)(2,1)S(1)} %get-tuple-element.62), channel_id=1, source_target_pairs={{0,2},{2,4},{4,6},{6,8},{8,10},{10,12},{12,14},{14,16},{16,18},{18... | collective-permute-start | bytes 196616 | tf_op jit(solution)/shard_map/ppermute | solution.py:16
  108.1 9.4 %collective-permute-start.13 = (bf16[64,512]{1,0:T(8,128)(2,1)S(1)}, bf16[64,512]{1,0:T(8,128)(2,1)S(1)}, u32[]{:S(2)}, u32[]{:S(2)}) collective-permute-start(bf16[64,512]{1,0:T(8,128)(2,1)S(1)} %get-tuple-element.63), channel_id=1, source_target_pairs={{2,0},{4,2},{6,4},{8,6},{10,8},{12,10},{14,12},{16,14},{18,16},{20... | collective-permute-start | bytes 196616 | tf_op jit(solution)/shard_map/ppermute | solution.py:19
  129.4 69.5 %copy-start.12 = (bf16[4,16,1024]{2,1,0:T(8,128)(2,1)S(1)}, bf16[4,16,1024]{2,1,0:T(8,128)(2,1)}, u32[]{:S(2)}) copy-start(bf16[4,16,1024]{2,1,0:T(8,128)(2,1)} %param.10) | copy-start | bytes 393220
  130.9 9.1 %collective-permute-start.14 = (f32[64,1]{1,0:T(8,128)S(1)}, f32[64,1]{1,0:T(8,128)S(1)}, u32[]{:S(2)}, u32[]{:S(2)}) collective-permute-start(f32[64,1]{1,0:T(8,128)S(1)} %get-tuple-element.26), channel_id=1, source_target_pairs={{0,2},{2,4},{4,6},{6,8},{8,10},{10,12},{12,14},{14,16},{16,18},{18... | collective-permute-start | bytes 776 | tf_op jit(solution)/shard_map/ppermute | solution.py:16
  131.0 9.6 %collective-permute-start.15 = (f32[64,1]{1,0:T(8,128)S(1)}, f32[64,1]{1,0:T(8,128)S(1)}, u32[]{:S(2)}, u32[]{:S(2)}) collective-permute-start(f32[64,1]{1,0:T(8,128)S(1)} %get-tuple-element.27), channel_id=1, source_target_pairs={{2,0},{4,2},{6,4},{8,6},{10,8},{12,10},{14,12},{16,14},{18,16},{20... | collective-permute-start | bytes 776 | tf_op jit(solution)/shard_map/ppermute | solution.py:19
  190.5 384.3 %reduce-scatter.5.cloned.1.call-start = ((), (), s32[]{:S(2)}) async-start(), calls=%async_computation.7 | async-start | bytes 49152 | tf_op jit(solution)/shard_map/reduce_scatter | solution.py:78
  199.5 9.2 %copy-start.2 = (f32[64,4096]{1,0:T(8,128)}, f32[64,4096]{1,0:T(8,128)S(1)}, u32[]{:S(2)}) copy-start(f32[64,4096]{1,0:T(8,128)S(1)} %add.82) | copy-start | bytes 3145732
  199.6 9.1 %collective-permute-start.16 = (f32[64,1]{1,0:T(8,128)S(1)}, f32[64,1]{1,0:T(8,128)S(1)}, u32[]{:S(2)}, u32[]{:S(2)}) collective-permute-start(f32[64,1]{1,0:T(8,128)S(1)} %get-tuple-element.24), channel_id=1, source_target_pairs={{0,2},{2,4},{4,6},{6,8},{8,10},{10,12},{12,14},{14,16},{16,18},{18... | collective-permute-start | bytes 776 | tf_op jit(solution)/shard_map/ppermute | solution.py:16
  199.6 9.1 %collective-permute-start.17 = (f32[64,1]{1,0:T(8,128)S(1)}, f32[64,1]{1,0:T(8,128)S(1)}, u32[]{:S(2)}, u32[]{:S(2)}) collective-permute-start(f32[64,1]{1,0:T(8,128)S(1)} %get-tuple-element.25), channel_id=1, source_target_pairs={{2,0},{4,2},{6,4},{8,6},{10,8},{12,10},{14,12},{16,14},{18,16},{20... | collective-permute-start | bytes 776 | tf_op jit(solution)/shard_map/ppermute | solution.py:19
  382.0 9.5 %collective-permute-start.18 = (bf16[64,512]{1,0:T(8,128)(2,1)S(1)}, bf16[64,512]{1,0:T(8,128)(2,1)S(1)}, u32[]{:S(2)}, u32[]{:S(2)}) collective-permute-start(bf16[64,512]{1,0:T(8,128)(2,1)S(1)} %get-tuple-element.56), channel_id=1, source_target_pairs={{0,2},{2,4},{4,6},{6,8},{8,10},{10,12},{12,14},{14,16},{16,18},{18... | collective-permute-start | bytes 196616 | tf_op jit(solution)/shard_map/ppermute | solution.py:16
  382.1 9.5 %collective-permute-start.19 = (bf16[64,512]{1,0:T(8,128)(2,1)S(1)}, bf16[64,512]{1,0:T(8,128)(2,1)S(1)}, u32[]{:S(2)}, u32[]{:S(2)}) collective-permute-start(bf16[64,512]{1,0:T(8,128)(2,1)S(1)} %get-tuple-element.57), channel_id=1, source_target_pairs={{2,0},{4,2},{6,4},{8,6},{10,8},{12,10},{14,12},{16,14},{18,16},{20... | collective-permute-start | bytes 196616 | tf_op jit(solution)/shard_map/ppermute | solution.py:19
  405.0 33.7 %copy-start.7 = (f32[4,8,8,1024]{3,2,0,1:T(8,128)}, f32[4,8,8,1024]{3,2,0,1:T(8,128)S(1)}, u32[]{:S(2)}) copy-start(f32[4,8,8,1024]{3,2,0,1:T(8,128)S(1)} %copy.68) | copy-start | bytes 3145732
  405.1 9.1 %collective-permute-start.20 = (f32[64,1]{1,0:T(8,128)S(1)}, f32[64,1]{1,0:T(8,128)S(1)}, u32[]{:S(2)}, u32[]{:S(2)}) collective-permute-start(f32[64,1]{1,0:T(8,128)S(1)} %get-tuple-element.22), channel_id=1, source_target_pairs={{0,2},{2,4},{4,6},{6,8},{8,10},{10,12},{12,14},{14,16},{16,18},{18... | collective-permute-start | bytes 776 | tf_op jit(solution)/shard_map/ppermute | solution.py:16
  405.1 9.2 %collective-permute-start.21 = (f32[64,1]{1,0:T(8,128)S(1)}, f32[64,1]{1,0:T(8,128)S(1)}, u32[]{:S(2)}, u32[]{:S(2)}) collective-permute-start(f32[64,1]{1,0:T(8,128)S(1)} %get-tuple-element.23), channel_id=1, source_target_pairs={{2,0},{4,2},{6,4},{8,6},{10,8},{12,10},{14,12},{16,14},{18,16},{20... | collective-permute-start | bytes 776 | tf_op jit(solution)/shard_map/ppermute | solution.py:19
  415.0 9.5 %collective-permute-start.22 = (bf16[64,512]{1,0:T(8,128)(2,1)S(1)}, bf16[64,512]{1,0:T(8,128)(2,1)S(1)}, u32[]{:S(2)}, u32[]{:S(2)}) collective-permute-start(bf16[64,512]{1,0:T(8,128)(2,1)S(1)} %get-tuple-element.50), channel_id=1, source_target_pairs={{0,2},{2,4},{4,6},{6,8},{8,10},{10,12},{12,14},{14,16},{16,18},{18... | collective-permute-start | bytes 196616 | tf_op jit(solution)/shard_map/ppermute | solution.py:16
  415.1 9.4 %collective-permute-start.23 = (bf16[64,512]{1,0:T(8,128)(2,1)S(1)}, bf16[64,512]{1,0:T(8,128)(2,1)S(1)}, u32[]{:S(2)}, u32[]{:S(2)}) collective-permute-start(bf16[64,512]{1,0:T(8,128)(2,1)S(1)} %get-tuple-element.51), channel_id=1, source_target_pairs={{2,0},{4,2},{6,4},{8,6},{10,8},{12,10},{14,12},{16,14},{18,16},{20... | collective-permute-start | bytes 196616 | tf_op jit(solution)/shard_map/ppermute | solution.py:19
  440.2 9.1 %collective-permute-start.24 = (f32[64,1]{1,0:T(8,128)S(1)}, f32[64,1]{1,0:T(8,128)S(1)}, u32[]{:S(2)}, u32[]{:S(2)}) collective-permute-start(f32[64,1]{1,0:T(8,128)S(1)} %get-tuple-element.20), channel_id=1, source_target_pairs={{0,2},{2,4},{4,6},{6,8},{8,10},{10,12},{12,14},{14,16},{16,18},{18... | collective-permute-start | bytes 776 | tf_op jit(solution)/shard_map/ppermute | solution.py:16
  440.2 9.2 %collective-permute-start.25 = (f32[64,1]{1,0:T(8,128)S(1)}, f32[64,1]{1,0:T(8,128)S(1)}, u32[]{:S(2)}, u32[]{:S(2)}) collective-permute-start(f32[64,1]{1,0:T(8,128)S(1)} %get-tuple-element.21), channel_id=1, source_target_pairs={{2,0},{4,2},{6,4},{8,6},{10,8},{12,10},{14,12},{16,14},{18,16},{20... | collective-permute-start | bytes 776 | tf_op jit(solution)/shard_map/ppermute | solution.py:19
  450.1 9.5 %collective-permute-start.26 = (bf16[64,512]{1,0:T(8,128)(2,1)S(1)}, bf16[64,512]{1,0:T(8,128)(2,1)S(1)}, u32[]{:S(2)}, u32[]{:S(2)}) collective-permute-start(bf16[64,512]{1,0:T(8,128)(2,1)S(1)} %get-tuple-element.44), channel_id=1, source_target_pairs={{0,2},{2,4},{4,6},{6,8},{8,10},{10,12},{12,14},{14,16},{16,18},{18... | collective-permute-start | bytes 196616 | tf_op jit(solution)/shard_map/ppermute | solution.py:16
  450.2 9.7 %collective-permute-start.27 = (bf16[64,512]{1,0:T(8,128)(2,1)S(1)}, bf16[64,512]{1,0:T(8,128)(2,1)S(1)}, u32[]{:S(2)}, u32[]{:S(2)}) collective-permute-start(bf16[64,512]{1,0:T(8,128)(2,1)S(1)} %get-tuple-element.45), channel_id=1, source_target_pairs={{2,0},{4,2},{6,4},{8,6},{10,8},{12,10},{14,12},{16,14},{18,16},{20... | collective-permute-start | bytes 196616 | tf_op jit(solution)/shard_map/ppermute | solution.py:19
  474.1 9.3 %copy-start.6 = (f32[64,4096]{1,0:T(8,128)}, f32[64,4096]{1,0:T(8,128)S(1)}, u32[]{:S(2)}) copy-start(f32[64,4096]{1,0:T(8,128)S(1)} %add.88) | copy-start | bytes 3145732
  474.2 9.1 %collective-permute-start.28 = (f32[64,1]{1,0:T(8,128)S(1)}, f32[64,1]{1,0:T(8,128)S(1)}, u32[]{:S(2)}, u32[]{:S(2)}) collective-permute-start(f32[64,1]{1,0:T(8,128)S(1)} %get-tuple-element.18), channel_id=1, source_target_pairs={{0,2},{2,4},{4,6},{6,8},{8,10},{10,12},{12,14},{14,16},{16,18},{18... | collective-permute-start | bytes 776 | tf_op jit(solution)/shard_map/ppermute | solution.py:16
  474.2 9.2 %collective-permute-start.29 = (f32[64,1]{1,0:T(8,128)S(1)}, f32[64,1]{1,0:T(8,128)S(1)}, u32[]{:S(2)}, u32[]{:S(2)}) collective-permute-start(f32[64,1]{1,0:T(8,128)S(1)} %get-tuple-element.19), channel_id=1, source_target_pairs={{2,0},{4,2},{6,4},{8,6},{10,8},{12,10},{14,12},{16,14},{18,16},{20... | collective-permute-start | bytes 776 | tf_op jit(solution)/shard_map/ppermute | solution.py:19
  484.1 9.5 %collective-permute-start.30 = (bf16[64,512]{1,0:T(8,128)(2,1)S(1)}, bf16[64,512]{1,0:T(8,128)(2,1)S(1)}, u32[]{:S(2)}, u32[]{:S(2)}) collective-permute-start(bf16[64,512]{1,0:T(8,128)(2,1)S(1)} %get-tuple-element.38), channel_id=1, source_target_pairs={{0,2},{2,4},{4,6},{6,8},{8,10},{10,12},{12,14},{14,16},{16,18},{18... | collective-permute-start | bytes 196616 | tf_op jit(solution)/shard_map/ppermute | solution.py:16
  484.2 9.4 %collective-permute-start.31 = (bf16[64,512]{1,0:T(8,128)(2,1)S(1)}, bf16[64,512]{1,0:T(8,128)(2,1)S(1)}, u32[]{:S(2)}, u32[]{:S(2)}) collective-permute-start(bf16[64,512]{1,0:T(8,128)(2,1)S(1)} %get-tuple-element.39), channel_id=1, source_target_pairs={{2,0},{4,2},{6,4},{8,6},{10,8},{12,10},{14,12},{16,14},{18,16},{20... | collective-permute-start | bytes 196616 | tf_op jit(solution)/shard_map/ppermute | solution.py:19
  493.7 25.0 %copy-start.13 = (bf16[4,16,1024]{2,1,0:T(8,128)(2,1)S(1)}, bf16[4,16,1024]{2,1,0:T(8,128)(2,1)}, u32[]{:S(2)}) copy-start(bf16[4,16,1024]{2,1,0:T(8,128)(2,1)} %param.10) | copy-start | bytes 393220
  505.8 251.6 %copy-start.3 = (f32[64,4096]{1,0:T(8,128)S(1)}, f32[64,4096]{1,0:T(8,128)}, u32[]{:S(2)}) copy-start(f32[64,4096]{1,0:T(8,128)} %copy-done.2) | copy-start | bytes 3145732
  508.5 9.5 %copy-start.4 = (f32[64,4096]{1,0:T(8,128)}, f32[64,4096]{1,0:T(8,128)S(1)}, u32[]{:S(2)}) copy-start(f32[64,4096]{1,0:T(8,128)S(1)} %add.90) | copy-start | bytes 3145732
  508.6 9.1 %collective-permute-start.32 = (f32[64,1]{1,0:T(8,128)S(1)}, f32[64,1]{1,0:T(8,128)S(1)}, u32[]{:S(2)}, u32[]{:S(2)}) collective-permute-start(f32[64,1]{1,0:T(8,128)S(1)} %get-tuple-element.16), channel_id=1, source_target_pairs={{0,2},{2,4},{4,6},{6,8},{8,10},{10,12},{12,14},{14,16},{16,18},{18... | collective-permute-start | bytes 776 | tf_op jit(solution)/shard_map/ppermute | solution.py:16
  508.6 9.4 %collective-permute-start.33 = (f32[64,1]{1,0:T(8,128)S(1)}, f32[64,1]{1,0:T(8,128)S(1)}, u32[]{:S(2)}, u32[]{:S(2)}) collective-permute-start(f32[64,1]{1,0:T(8,128)S(1)} %get-tuple-element.17), channel_id=1, source_target_pairs={{2,0},{4,2},{6,4},{8,6},{10,8},{12,10},{14,12},{16,14},{18,16},{20... | collective-permute-start | bytes 776 | tf_op jit(solution)/shard_map/ppermute | solution.py:19
  577.4 9.2 %copy-start.9 = (f32[64,4096]{1,0:T(8,128)}, f32[64,4096]{1,0:T(8,128)S(1)}, u32[]{:S(2)}) copy-start(f32[64,4096]{1,0:T(8,128)S(1)} %add.92) | copy-start | bytes 3145732
  577.5 9.1 %collective-permute-start.34 = (f32[64,1]{1,0:T(8,128)S(1)}, f32[64,1]{1,0:T(8,128)S(1)}, u32[]{:S(2)}, u32[]{:S(2)}) collective-permute-start(f32[64,1]{1,0:T(8,128)S(1)} %get-tuple-element.14), channel_id=1, source_target_pairs={{0,2},{2,4},{4,6},{6,8},{8,10},{10,12},{12,14},{14,16},{16,18},{18... | collective-permute-start | bytes 776 | tf_op jit(solution)/shard_map/ppermute | solution.py:16
  577.5 9.1 %collective-permute-start.35 = (f32[64,1]{1,0:T(8,128)S(1)}, f32[64,1]{1,0:T(8,128)S(1)}, u32[]{:S(2)}, u32[]{:S(2)}) collective-permute-start(f32[64,1]{1,0:T(8,128)S(1)} %get-tuple-element.15), channel_id=1, source_target_pairs={{2,0},{4,2},{6,4},{8,6},{10,8},{12,10},{14,12},{16,14},{18,16},{20... | collective-permute-start | bytes 776 | tf_op jit(solution)/shard_map/ppermute | solution.py:19
Sparse Core Ops, SparseCore 0:
  190.6 7.4 reduce-scatter.2
  567.3 7.4 reduce-scatter.4
